TPU v7x, 32 devices: a whole 2x2x4 slice. The times are simulated.
32 devices in a mesh: groups: 2 (over x), seq: 16 (over z, y, core).
Axes of the slice: x: 2, y: 2, z: 4, core: 2. Of those that a mesh axis runs over, the one named last changes fastest.
Arguments:
- hidden: bfloat16 [16384, 4096], P(('groups', 'seq')), parts along dimension 0, may hold values from -6 to 6
- norm_gain: bfloat16 [4096], replicated, may hold values from 0.5 to 1.5
- w_query: bfloat16 [4096, 32], replicated, may hold values from -0.09375 to 0.09375
- w_key: bfloat16 [4096, 32], replicated, may hold values from -0.09375 to 0.09375
- conv_kernel: float32 [4, 32], replicated, may hold values from -3 to 3
- out_gain: bfloat16 [4096], replicated, may hold values from 0.5 to 1.5
Outputs:
- adapted: bfloat16 [16384, 4096], P(('groups', 'seq')), parts along dimension 0
There are 2 independent parts, one for each index of `groups`. A program takes and returns all parts, laid end to end along the dimension named above; an argument that names none is the same for every part. Nothing has to cross between parts.
All inputs are finite; a program needn't handle non-finite values.
Results may differ from a plain program's by a relative error of at most 0.0097.
Values may be sent and summed in bfloat16 or wider, within the bound.
A program may use at most 128 MiB of HBM per device.

v0:
```python
import jax
import jax.numpy as jnp
from jax import lax
from jax.sharding import PartitionSpec as P

epsilon = 1e-06


def from_behind(shard, axis, by):
    length = lax.axis_size(axis)
    pairs = [(i, i + by) for i in range(length) if 0 <= i + by < length]
    return lax.ppermute(shard, axis, pairs)


def carried_in(value, axis, join, neutral):
    count, mine = (lax.axis_size(axis), lax.axis_index(axis))
    pieces = lax.all_gather(value, axis)
    subtotal = jnp.full_like(value, 0) + jnp.asarray(neutral, value.dtype)

    def lap(position, subtotal):
        longer = join(subtotal, pieces[position])
        return jnp.where(position < mine, longer, subtotal)

    return lax.fori_loop(0, count - 1, lap, subtotal)


def rms_scale(values, gain):
    floats = values.astype(jnp.float32)
    inv_rms = lax.rsqrt(jnp.mean(floats * floats, axis=-1, keepdims=True) + epsilon)
    return floats * inv_rms * gain.astype(jnp.float32)


def add_states(earlier, later):
    return earlier + later


def shards(hidden, norm_gain, w_query, w_key, conv_kernel, out_gain):
    tok_rows = hidden.shape[0]
    width = conv_kernel.shape[0]
    normed = rms_scale(hidden, norm_gain).astype(jnp.bfloat16)
    queries = jnp.dot(normed, w_query, preferred_element_type=jnp.float32).astype(jnp.bfloat16)
    raw_keys = jnp.dot(normed, w_key, preferred_element_type=jnp.float32).astype(jnp.bfloat16)
    tail_rows = raw_keys[tok_rows - (width - 1) :]
    previous = from_behind(tail_rows, "seq", 1)
    extended = jnp.concatenate([previous, raw_keys], axis=0)
    summed = jnp.zeros((tok_rows, raw_keys.shape[1]), jnp.float32)
    for offset in range(width):
        start = width - 1 - offset
        summed = summed + conv_kernel[offset][None, :] * extended[start : start + tok_rows].astype(
            jnp.float32
        )
    key_rows = summed.astype(jnp.bfloat16)
    own_state = lax.dot_general(
        key_rows, hidden, (((0,), (0,)), ((), ())), preferred_element_type=jnp.float32
    )
    prefix_state = carried_in(own_state, "seq", add_states, jnp.zeros_like(own_state))
    prefix_low = prefix_state.astype(jnp.bfloat16)
    carried = jnp.dot(queries, prefix_low, preferred_element_type=jnp.float32)
    positions = jnp.arange(tok_rows, dtype=jnp.int32)
    causal = positions[:, None] >= positions[None, :]
    scores = lax.dot_general(
        queries, key_rows, (((1,), (1,)), ((), ())), preferred_element_type=jnp.float32
    )
    scores = jnp.where(causal, scores, jnp.zeros_like(scores)).astype(jnp.bfloat16)
    local_term = jnp.dot(scores, hidden, preferred_element_type=jnp.float32)
    mixed = carried + local_term
    return rms_scale(mixed, out_gain).astype(jnp.bfloat16)


def solution(mesh):
    placed = (P(("groups", "seq"), None), P(), P(), P(), P(), P())
    return jax.shard_map(
        shards, mesh=mesh, in_specs=placed, out_specs=P(("groups", "seq"), None), check_vma=False
    )
```

profile of v0, /device:TPU:0, one launch (start us, length us, event | category | flops | bytes accessed | tf_op | source)
XLA Modules:
  0.0 132.3 jit_solution(395027324333595462)
XLA Ops:
  6.5 0.0 copy-start
  6.5 0.0 all-gather.3.cloned.1.call-start
  6.5 3.2 %fusion = f32[512]{0:T(512)S(1)} fusion(bf16[512,4096]{1,0:T(8,128)(2,1)} %param.8), kind=kLoop, calls=%fused_computation.3 | loop fusion | flops 6290944 | bytes 4196352 | tf_op jit(solution)/shard_map/reduce_sum | solution.py:29
  9.8 0.7 convert_element_type.43
  10.5 0.0 copy-done
  10.5 3.7 %fusion.12 = bf16[512,32]{0,1:T(8,128)(2,1)S(1)} fusion(bf16[4096,32]{0,1:T(8,128)(2,1)S(1)} %copy-done, bf16[512,4096]{1,0:T(8,128)(2,1)} %param.8, f32[4096]{0:T(1024)S(1)} %convert_element_type.43, f32[512]{0:T(512)S(1)} %add_rsqrt_fusion.1), kind=kOutput, calls=%fused_computation.15 | convolution fusion | flops 142622720 | bytes 4507648 | tf_op jit(solution)/shard_map/dot_general | solution.py:42
  14.2 0.1 slice.32
  14.2 2.4 %collective-permute-start = (bf16[3,32]{0,1:T(8,128)(2,1)S(1)}, bf16[3,32]{0,1:T(8,128)(2,1)S(1)}, u32[]{:S(2)}, u32[]{:S(2)}) collective-permute-start(bf16[3,32]{0,1:T(8,128)(2,1)S(1)} %slice.32), channel_id=1, source_target_pairs={{0,1},{1,2},{2,3},{3,4},{4,5},{5,6},{6,7},{7,8},{8,9},{9,10},{10,1... | collective-permute-start | bytes 584 | tf_op jit(solution)/shard_map/ppermute | solution.py:12
  16.6 0.8 collective-permute-done
  17.4 1.7 %fusion.20 = f32[32,4096]{1,0:T(8,128)} fusion(bf16[512,4096]{1,0:T(8,128)(2,1)S(1)} %copy-done.1, bf16[512,32]{0,1:T(8,128)(2,1)S(1)} %fusion.12, bf16[3,32]{0,1:T(8,128)(2,1)S(1)} %collective-permute-done, f32[32]{0:T(128)S(1)} %get-tuple-element.110, f32[32]{0:T(128)S(1)} %get-tuple-element.111, f32[32]{0:T(128)S(1)} %get-tuple-element.109, ...), kind=kOutput, calls=%fused_computation.34 | convolution fusion | flops 134561792 | bytes 4752064 | tf_op jit(solution)/shard_map/dot_general | solution.py:53
  19.1 0.0 all-gather.3.cloned.1.call-update
  19.2 3.6 %fusion.9 = bf16[512,32]{0,1:T(8,128)(2,1)S(1)} fusion(bf16[4096,32]{0,1:T(8,128)(2,1)S(1)} %copy-done.4, bf16[512,4096]{1,0:T(8,128)(2,1)} %param.8, f32[4096]{0:T(1024)S(1)} %convert_element_type.43, f32[512]{0:T(512)S(1)} %add_rsqrt_fusion.1), kind=kOutput, calls=%fused_computation.14 | convolution fusion | flops 142622720 | bytes 4507648 | tf_op jit(solution)/shard_map/dot_general | solution.py:41
  22.8 8.0 %fusion.4 = f32[512,4096]{1,0:T(8,128)} fusion(bf16[512,4096]{1,0:T(8,128)(2,1)} %param.8, bf16[512,32]{0,1:T(8,128)(2,1)S(1)} %fusion.9, bf16[512,32]{0,1:T(8,128)(2,1)S(1)} %fusion.12, bf16[3,32]{0,1:T(8,128)(2,1)S(1)} %collective-permute-done, f32[32]{0:T(128)S(1)} %get-tuple-element.110, f32[32]{0:T(128)S(1)} %get-tuple-element.111, ...), kind=kOutput, calls=%fused_computation.11 | convolution fusion | flops 2165391360 | bytes 12649152 | tf_op jit(solution)/shard_map/dot_general | solution.py:65
  30.8 67.9 %all-gather.3.cloned.1.call-done = f32[512,4096]{1,0:T(8,128)} async-done(((f32[32,4096]{1,0:T(8,128)}), f32[512,4096]{1,0:T(8,128)}) %all-gather.3.cloned.1.call-update) | async-done | bytes 8388624 | tf_op jit(solution)/shard_map/all_gather | solution.py:17
  98.7 18.6 %while.14 = (s32[]{:T(128)}, f32[32,4096]{1,0:T(8,128)S(1)}, s32[]{:T(128)}, f32[16,32,4096]{2,1,0:T(8,128)}, s32[]{:T(128)}, /*index=5*/s32[]{:T(128)}) while((s32[]{:T(128)}, f32[32,4096]{1,0:T(8,128)S(1)}, s32[]{:T(128)}, f32[16,32,4096]{2,1,0:T(8,128)}, s32[]{:T(128)}, /*index=5*/s32[]{:T(128)}) %tuple.41), condition=%wide.region_2.3_spmd.clone, body=%wide.region_1.2_spmd.clone.sunk | while | flops 393220 | bytes 1572965 | solution.py:24
  98.7 1.2 add_select_fusion.2
  99.9 1.2 add_select_fusion.2
  101.1 1.2 add_select_fusion.2
  102.4 1.2 add_select_fusion.2
  103.6 1.2 add_select_fusion.2
  104.9 1.2 add_select_fusion.2
  106.1 1.2 add_select_fusion.2
  107.3 1.2 add_select_fusion.2
  108.6 1.2 add_select_fusion.2
  109.8 1.2 add_select_fusion.2
  111.1 1.2 add_select_fusion.2
  112.3 1.2 add_select_fusion.2
  113.5 1.2 add_select_fusion.2
  114.8 1.2 add_select_fusion.2
  116.0 1.2 add_select_fusion.2
  117.2 4.7 %multiply_reduce_fusion = (f32[512]{0:T(512)S(1)}, f32[512,4096]{1,0:T(8,128)S(1)}) fusion(f32[512,4096]{1,0:T(8,128)} %fusion.4, bf16[512,32]{0,1:T(8,128)(2,1)S(1)} %fusion.9, f32[32,4096]{1,0:T(8,128)S(1)} %get-tuple-element.84), kind=kOutput, calls=%fused_computation.7 | convolution fusion | flops 140639744 | bytes 17336320 | tf_op jit(solution)/shard_map/dot_general | solution.py:58
  122.0 3.5 %multiply_convert_fusion = bf16[512,4096]{1,0:T(8,128)(2,1)} fusion(f32[512,4096]{1,0:T(8,128)S(1)} %get-tuple-element.113, f32[4096]{0:T(1024)S(1)} %convert_element_type.54, f32[512]{0:T(512)S(1)} %add_rsqrt_fusion), kind=kLoop, calls=%fused_computation.6 | loop fusion | flops 6291456 | bytes 12601344 | tf_op jit(solution)/shard_map/convert_element_type | solution.py:67
  (13 shorter events, 0.0 us)
Async XLA Ops:
  6.5 4.0 %copy-start = (bf16[4096,32]{0,1:T(8,128)(2,1)S(1)}, bf16[4096,32]{0,1:T(8,128)(2,1)}, u32[]{:S(2)}) copy-start(bf16[4096,32]{0,1:T(8,128)(2,1)} %param.11) | copy-start | bytes 786436
  6.5 10.1 %copy-start.3 = (f32[4,32]{1,0:T(4,128)S(1)}, f32[4,32]{1,0:T(4,128)}, u32[]{:S(2)}) copy-start(f32[4,32]{1,0:T(4,128)} %param.12) | copy-start | bytes 1540
  6.5 92.1 %all-gather.3.cloned.1.call-start = ((), (), s32[]{:S(2)}) async-start(), calls=%async_computation | async-start | bytes 8912896 | tf_op jit(solution)/shard_map/all_gather | solution.py:17
  6.5 10.9 %copy-start.1 = (bf16[512,4096]{1,0:T(8,128)(2,1)S(1)}, bf16[512,4096]{1,0:T(8,128)(2,1)}, u32[]{:S(2)}) copy-start(bf16[512,4096]{1,0:T(8,128)(2,1)} %param.8) | copy-start | bytes 12582916
  10.5 8.6 %copy-start.2 = (bf16[4096]{0:T(1024)(128)(2,1)S(1)}, bf16[4096]{0:T(1024)(128)(2,1)}, u32[]{:S(2)}) copy-start(bf16[4096]{0:T(1024)(128)(2,1)} %param.13) | copy-start | bytes 24580
  10.5 8.6 %copy-start.4 = (bf16[4096,32]{0,1:T(8,128)(2,1)S(1)}, bf16[4096,32]{0,1:T(8,128)(2,1)}, u32[]{:S(2)}) copy-start(bf16[4096,32]{0,1:T(8,128)(2,1)} %param.10) | copy-start | bytes 786436
  14.2 3.2 %collective-permute-start = (bf16[3,32]{0,1:T(8,128)(2,1)S(1)}, bf16[3,32]{0,1:T(8,128)(2,1)S(1)}, u32[]{:S(2)}, u32[]{:S(2)}) collective-permute-start(bf16[3,32]{0,1:T(8,128)(2,1)S(1)} %slice.32), channel_id=1, source_target_pairs={{0,1},{1,2},{2,3},{3,4},{4,5},{5,6},{6,7},{7,8},{8,9},{9,10},{10,1... | collective-permute-start | bytes 584 | tf_op jit(solution)/shard_map/ppermute | solution.py:12
Sparse Core Ops, SparseCore 0:
  19.2 79.3 all-gather.2
where the time goes:
time: 133 us; the launch traced here: 132 us
  waiting for transfers between devices  68.7 us (52%)
  other arithmetic  25.7 us (19%)
  matrix products  21.7 us (16%)
  between operations  13.5 us (10%)
  starting transfers between devices  2.35 us (2%)
    all_gather x1, waiting for transfers between devices, carried_in(): pieces = lax.all_gather(value, axis)  67.9 us
    select_n x15, other arithmetic, lap(): return jnp.where(position < mine, longer, subtotal)  18.2 us
    dot_general x1, matrix products, shards(): local_term = jnp.dot(scores, hidden, preferred_element_type=jnp.float32)  8.01 us
    dot_general x1, matrix products, shards(): carried = jnp.dot(queries, prefix_low, preferred_element_type=jnp.float32)  4.74 us
    dot_general x1, matrix products, shards(): jnp.dot(normed, w_key, preferred_element_type=jnp.float32)  3.65 us
    dot_general x1, matrix products, shards(): jnp.dot(normed, w_query, preferred_element_type=jnp.float32)  3.61 us
    convert_element_type x1, other arithmetic, shards(): return rms_scale(mixed, out_gain).astype(jnp.bfloat16)  3.47 us
    reduce_sum x1, other arithmetic, rms_scale(): jnp.mean(floats * floats, axis=-1, keepdims=True) + epsilon  3.23 us
  transfers between devices with their start and end apart: 2, of which 2 were waited for; matrix products, arithmetic and copies ran while one was open for 9% of the time, Pallas kernels for 0%

commit v1 on v0

v1 whole, which is shorter than its diff:
```python
import functools

import jax
import jax.numpy as jnp
from jax import lax
from jax.experimental import pallas as pl
from jax.experimental.pallas import tpu as pltpu
from jax.sharding import PartitionSpec as P

epsilon = 1e-06
MESH = pl.DeviceIdType.MESH
F32 = jnp.float32
BF16 = jnp.bfloat16


def state_kernel(n, team, hidden, gain, w_key, w_query, conv, local_out, q_out, pref_out,
                 hbuf, wcat, rk, tail, halo, kbuf, qbuf, sbuf, own, got, total, got2, acc, pbuf,
                 load_sem, halo_sem, send1, recv1, send2, recv2, send3, recv3):
    rows, width = hbuf.shape
    rank = w_key.shape[0]
    taps = conv.shape[0]
    part = width // team
    planes = n // team
    chunks = load_sem.shape[0]
    step = rows // chunks
    me = lax.axis_index("seq")
    pos = lax.rem(me, team)
    plane = me // team
    order = [chunks - 1] + list(range(chunks - 1))

    def load(c):
        span = pl.ds(c * step, step)
        return pltpu.make_async_copy(hidden.at[span], hbuf.at[span], load_sem.at[c])

    for c in order:
        load(c).start()

    barrier = pltpu.get_barrier_semaphore()

    def greet(other):
        pl.semaphore_signal(barrier, inc=1, device_id={"seq": other}, device_id_type=MESH)

    for j in range(1, n):
        greet(lax.rem(me + j, n))

    scale = gain[...].astype(F32).reshape(1, width)
    wcat[pl.ds(0, rank), :] = (w_key[...].astype(F32) * scale).astype(BF16)
    wcat[pl.ds(rank, rank), :] = (w_query[...].astype(F32) * scale).astype(BF16)
    halo_copy = pltpu.make_async_remote_copy(
        src_ref=tail, dst_ref=halo, send_sem=halo_sem.at[0], recv_sem=halo_sem.at[1],
        device_id={"seq": jnp.minimum(me + 1, n - 1)}, device_id_type=MESH)

    for c in order:
        load(c).wait()
        h = hbuf[pl.ds(c * step, step), :]
        hf = h.astype(F32)
        inv = lax.rsqrt(jnp.sum(hf * hf, axis=1, keepdims=True) * (1.0 / width) + epsilon)
        proj = lax.dot_general(h, wcat[...], (((1,), (1,)), ((), ())), preferred_element_type=F32)
        proj = (proj * inv).astype(BF16)
        qbuf[pl.ds(c * step, step), :] = proj[:, rank:]
        keys = proj[:, :rank].astype(F32)
        rk[pl.ds(8 + c * step, step), :] = keys
        if c == chunks - 1:
            tail[:, :rank] = keys[step - 8:, :]
            tail[:, rank:] = jnp.zeros((8, tail.shape[1] - rank), F32)
            pl.semaphore_wait(barrier, n - 1)

            @pl.when(me < n - 1)
            def _():
                halo_copy.start()

    @pl.when(me > 0)
    def _():
        halo_copy.wait_recv()
        rk[pl.ds(0, 8), :] = halo[:, :rank]

    @pl.when(me == 0)
    def _():
        rk[pl.ds(0, 8), :] = jnp.zeros((8, rank), F32)

    summed = conv[0:1, :] * rk[pl.ds(8, rows), :]
    for j in range(1, taps):
        summed = summed + conv[j:j + 1, :] * rk[pl.ds(8 - j, rows), :]
    kbuf[...] = summed.astype(BF16)
    keys_t = summed.T.astype(BF16)

    for p in range(team):
        own[p] = jnp.dot(keys_t, hbuf[:, p * part:(p + 1) * part], preferred_element_type=F32).astype(BF16)

    def phase1(j):
        to = lax.rem(pos + j, team)
        return pltpu.make_async_remote_copy(
            src_ref=own.at[to], dst_ref=got.at[pos], send_sem=send1.at[j - 1], recv_sem=recv1.at[j - 1],
            device_id={"seq": plane * team + to}, device_id_type=MESH)

    def phase2(k):
        return pltpu.make_async_remote_copy(
            src_ref=total, dst_ref=got2.at[k - 1], send_sem=send2.at[k - 1], recv_sem=recv2.at[k - 1],
            device_id={"seq": lax.rem(plane + k, planes) * team + pos}, device_id_type=MESH)

    def phase3(j):
        to = lax.rem(pos + j, team)
        return pltpu.make_async_remote_copy(
            src_ref=pbuf.at[to], dst_ref=pref_out.at[pos], send_sem=send3.at[j - 1], recv_sem=recv3.at[j - 1],
            device_id={"seq": plane * team + to}, device_id_type=MESH)

    for j in range(1, team):
        phase1(j).start()
    got[pos] = own[pos]

    q = qbuf[...]
    q_out[...] = q
    scores = lax.dot_general(q, kbuf[...], (((1,), (1,)), ((), ())), preferred_element_type=F32)
    at_row = lax.broadcasted_iota(jnp.int32, scores.shape, 0)
    at_col = lax.broadcasted_iota(jnp.int32, scores.shape, 1)
    sbuf[...] = jnp.where(at_row >= at_col, scores, 0.0).astype(BF16)

    halves = 2
    half = rows // halves
    tile = 512

    def local(b):
        depth = (b + 1) * half

        @pl.loop(0, width // tile)
        def _(t):
            cols = pl.ds(pl.multiple_of(t * tile, tile), tile)
            local_out[pl.ds(b * half, half), cols] = jnp.dot(
                sbuf[pl.ds(b * half, half), pl.ds(0, depth)], hbuf[pl.ds(0, depth), cols],
                preferred_element_type=F32)

    local(0)

    for j in range(1, team):
        phase1(j).wait()
    total[...] = sum(got[p].astype(F32) for p in range(team)).astype(BF16)
    for k in range(1, planes):
        @pl.when(plane + k < planes)
        def _():
            phase2(k).start()

    local(1)

    acc[...] = jnp.zeros_like(acc)
    for k in range(1, planes):
        @pl.when(plane >= k)
        def _():
            phase2(k).wait_recv()
            acc[...] += got2[k - 1].astype(F32)

    running = acc[...]
    for p in range(team):
        pbuf[p] = running.astype(BF16)
        if p < team - 1:
            running = running + got[p].astype(F32)
    for j in range(1, team):
        phase3(j).start()
    pref_out[pos] = pbuf[pos]
    for j in range(1, team):
        phase3(j).wait()
    for k in range(1, planes):
        @pl.when(plane + k < planes)
        def _():
            phase2(k).wait_send()

    @pl.when(me < n - 1)
    def _():
        halo_copy.wait_send()


def finish_kernel(local, q, pref, gain, out, mixed, done, sem):
    team, _, part = pref.shape
    width = team * part
    blocks = sem.shape[0]
    block = local.shape[0] // blocks
    scale = gain[...].astype(F32).reshape(1, width)
    copies = []
    for b in range(blocks):
        span = pl.ds(b * block, block)
        squares = jnp.zeros((block, 1), F32)
        for p in range(team):
            cols = pl.ds(p * part, part)
            m = local[span, cols] + jnp.dot(q[span, :], pref[p], preferred_element_type=F32)
            mixed[:, cols] = m
            squares = squares + jnp.sum(m * m, axis=1, keepdims=True)
        inv = lax.rsqrt(squares * (1.0 / width) + epsilon)
        done[span, :] = (mixed[...] * inv * scale).astype(BF16)
        copies.append(pltpu.make_async_copy(done.at[span], out.at[span], sem.at[b]))
        copies[-1].start()
    for copy in copies:
        copy.wait()


def shards(n, hidden, norm_gain, w_query, w_key, conv_kernel, out_gain):
    rows, width = hidden.shape
    taps, rank = conv_kernel.shape
    team = 4
    planes = n // team
    part = width // team
    chunks = 4
    vmem = pl.BlockSpec(memory_space=pltpu.VMEM)
    anyspace = pl.BlockSpec(memory_space=pltpu.HBM)
    dma = pltpu.SemaphoreType.DMA
    later = max(planes - 1, 1)
    local, q, pref = pl.pallas_call(
        functools.partial(state_kernel, n, team),
        out_shape=(jax.ShapeDtypeStruct((rows, width), F32),
                   jax.ShapeDtypeStruct((rows, rank), BF16),
                   jax.ShapeDtypeStruct((team, rank, part), BF16)),
        in_specs=[anyspace, vmem, vmem, vmem, vmem],
        out_specs=(vmem, vmem, vmem),
        scratch_shapes=[
            pltpu.VMEM((rows, width), BF16),
            pltpu.VMEM((2 * rank, width), BF16),
            pltpu.VMEM((rows + 8, rank), F32),
            pltpu.VMEM((8, 128), F32),
            pltpu.VMEM((8, 128), F32),
            pltpu.VMEM((rows, rank), BF16),
            pltpu.VMEM((rows, rank), BF16),
            pltpu.VMEM((rows, rows), BF16),
            pltpu.VMEM((team, rank, part), BF16),
            pltpu.VMEM((team, rank, part), BF16),
            pltpu.VMEM((rank, part), BF16),
            pltpu.VMEM((later, rank, part), BF16),
            pltpu.VMEM((rank, part), F32),
            pltpu.VMEM((team, rank, part), BF16),
            dma((chunks,)), dma((2,)),
            dma((team - 1,)), dma((team - 1,)),
            dma((later,)), dma((later,)),
            dma((team - 1,)), dma((team - 1,)),
        ],
        compiler_params=pltpu.CompilerParams(
            collective_id=0, has_side_effects=True, vmem_limit_bytes=32 * 1024 * 1024),
    )(hidden, norm_gain, w_key.T, w_query.T, conv_kernel)

    return pl.pallas_call(
        finish_kernel,
        out_shape=jax.ShapeDtypeStruct((rows, width), BF16),
        in_specs=[vmem, vmem, vmem, vmem],
        out_specs=anyspace,
        scratch_shapes=[pltpu.VMEM((rows // 8, width), F32), pltpu.VMEM((rows, width), BF16), dma((8,))],
        compiler_params=pltpu.CompilerParams(vmem_limit_bytes=32 * 1024 * 1024),
    )(local, q, pref, out_gain)


def solution(mesh):
    placed = (P(("groups", "seq"), None), P(), P(), P(), P(), P())
    return jax.shard_map(
        functools.partial(shards, mesh.shape["seq"]), mesh=mesh, in_specs=placed,
        out_specs=P(("groups", "seq"), None), check_vma=False
    )
```

time: 133 us -> 32.5 us (0.24)
  the two profiles are of different devices: /device:TPU:0 before, /device:TPU:25 now
where the time goes in v1:
time: 32.5 us; the launch traced here: 32.3 us
  Pallas kernels  26.8 us (82%)
  local copies, waits for them, and re-layouts  5.47 us (17%)
    pallas_call x1, Pallas kernels, shards(): pl.pallas_call(functools.partial(state_kernel, n, team), out_shape=(jax.S...  23.4 us
    unnamed x12, local copies, waits for them, and re-layouts  5.47 us
    pallas_call x1, Pallas kernels, shards(): pl.pallas_call(finish_kernel, out_shape=jax.ShapeDtypeStruct((rows, width...  3.4 us

profile of v1, /device:TPU:25, one launch (start us, length us, event | category | flops | bytes accessed | tf_op | source)
XLA Modules:
  0.0 32.3 jit_solution(485234024337752188)
XLA Ops:
  0.0 0.0 copy-start
  0.0 2.2 %copy-done = bf16[512,4096]{1,0:T(8,128)(2,1)S(1)} copy-done((bf16[512,4096]{1,0:T(8,128)(2,1)S(1)}, bf16[512,4096]{1,0:T(8,128)(2,1)}, u32[]{:S(2)}) %copy-start) | copy-done | bytes 4194328
  2.2 0.0 copy-start.1
  2.2 0.9 %copy-done.1 = bf16[4096,32]{0,1:T(8,128)(2,1)S(1)} copy-done((bf16[4096,32]{0,1:T(8,128)(2,1)S(1)}, bf16[4096,32]{0,1:T(8,128)(2,1)}, u32[]{:S(2)}) %copy-start.1) | copy-done | bytes 262168
  3.1 0.0 copy-start.2
  3.1 0.9 %copy-done.2 = bf16[4096,32]{0,1:T(8,128)(2,1)S(1)} copy-done((bf16[4096,32]{0,1:T(8,128)(2,1)S(1)}, bf16[4096,32]{0,1:T(8,128)(2,1)}, u32[]{:S(2)}) %copy-start.2) | copy-done | bytes 262168
  4.1 0.0 copy-start.3
  4.1 0.7 %copy-done.3 = bf16[4096]{0:T(1024)(128)(2,1)S(1)} copy-done((bf16[4096]{0:T(1024)(128)(2,1)S(1)}, bf16[4096]{0:T(1024)(128)(2,1)}, u32[]{:S(2)}) %copy-start.3) | copy-done | bytes 8216
  4.8 0.0 copy-start.5
  4.8 0.7 %copy-done.5 = f32[4,32]{1,0:T(4,128)S(1)} copy-done((f32[4,32]{1,0:T(4,128)S(1)}, f32[4,32]{1,0:T(4,128)}, u32[]{:S(2)}) %copy-start.5) | copy-done | bytes 536
  5.5 0.0 copy-start.4
  5.5 23.4 %shard_map.64 = (f32[512,4096]{1,0:T(8,128)S(1)}, bf16[512,32]{1,0:T(8,128)(2,1)S(1)}, bf16[4,32,1024]{2,1,0:T(8,128)(2,1)S(1)}) custom-call(bf16[512,4096]{1,0:T(8,128)(2,1)S(1)} %copy-done, bf16[4096]{0:T(1024)(128)(2,1)S(1)} %copy-done.3, bf16[32,4096]{1,0:T(8,128)(2,1)S(1)} %bitcast.2, bf16[32,4096]{1,0:T(8,128)(2,1)S(1)} %bitcast.3, f32[4,32]{1,0:T(4,128)S(1)} %copy-done.5), custom_call_target="tpu_custom_call" | custom-call | tf_op jit(solution)/shard_map/pallas_call | solution.py:205
  28.9 0.0 copy-done.4
  28.9 3.4 %shard_map.65 = bf16[512,4096]{1,0:T(8,128)(2,1)} custom-call(f32[512,4096]{1,0:T(8,128)S(1)} %get-tuple-element.8.local, bf16[512,32]{1,0:T(8,128)(2,1)S(1)} %get-tuple-element.9.q, bf16[4,32,1024]{2,1,0:T(8,128)(2,1)S(1)} %get-tuple-element.10.pref, bf16[4096]{0:T(1024)(128)(2,1)S(1)} %copy-done.4), custom_call_target="tpu_custom_call" | custom-call | tf_op jit(solution)/shard_map/pallas_call | solution.py:236
Async XLA Ops:
  0.0 2.2 %copy-start = (bf16[512,4096]{1,0:T(8,128)(2,1)S(1)}, bf16[512,4096]{1,0:T(8,128)(2,1)}, u32[]{:S(2)}) copy-start(bf16[512,4096]{1,0:T(8,128)(2,1)} %hidden.1) | copy-start | bytes 12582916
  2.2 0.9 %copy-start.1 = (bf16[4096,32]{0,1:T(8,128)(2,1)S(1)}, bf16[4096,32]{0,1:T(8,128)(2,1)}, u32[]{:S(2)}) copy-start(bf16[4096,32]{0,1:T(8,128)(2,1)} %param.9) | copy-start | bytes 786436
  3.1 0.9 %copy-start.2 = (bf16[4096,32]{0,1:T(8,128)(2,1)S(1)}, bf16[4096,32]{0,1:T(8,128)(2,1)}, u32[]{:S(2)}) copy-start(bf16[4096,32]{0,1:T(8,128)(2,1)} %param.8) | copy-start | bytes 786436
  4.1 0.7 %copy-start.3 = (bf16[4096]{0:T(1024)(128)(2,1)S(1)}, bf16[4096]{0:T(1024)(128)(2,1)}, u32[]{:S(2)}) copy-start(bf16[4096]{0:T(1024)(128)(2,1)} %gain.2) | copy-start | bytes 24580
  4.8 0.7 %copy-start.5 = (f32[4,32]{1,0:T(4,128)S(1)}, f32[4,32]{1,0:T(4,128)}, u32[]{:S(2)}) copy-start(f32[4,32]{1,0:T(4,128)} %conv.1) | copy-start | bytes 1540
  5.5 23.4 %copy-start.4 = (bf16[4096]{0:T(1024)(128)(2,1)S(1)}, bf16[4096]{0:T(1024)(128)(2,1)}, u32[]{:S(2)}) copy-start(bf16[4096]{0:T(1024)(128)(2,1)} %gain.3) | copy-start | bytes 24580

commit v2 on v1

--- a/solution.py
+++ b/solution.py
@@ -13,13 +13,13 @@
 BF16 = jnp.bfloat16
 
 
-def state_kernel(n, team, hidden, gain, w_key, w_query, conv, local_out, q_out, pref_out,
-                 hbuf, wcat, rk, tail, halo, kbuf, qbuf, sbuf, own, got, total, got2, acc, pbuf,
-                 load_sem, halo_sem, send1, recv1, send2, recv2, send3, recv3):
+def state_kernel(n, team, pieces, hidden, gain_in, w_key_in, w_query_in, conv_in, local_out, q_out, pref_out,
+                 hbuf, gain, w_key, w_query, conv, wcat, rk, tail, halo, kbuf, qbuf, sbuf, own, got, total, got2, acc, pbuf,
+                 small_sem, load_sem, halo_sem, send1, recv1, send2, recv2, send3, recv3):
     rows, width = hbuf.shape
     rank = w_key.shape[0]
     taps = conv.shape[0]
-    part = width // team
+    part = width // (team * pieces)
     planes = n // team
     chunks = load_sem.shape[0]
     step = rows // chunks
@@ -32,6 +32,10 @@
         span = pl.ds(c * step, step)
         return pltpu.make_async_copy(hidden.at[span], hbuf.at[span], load_sem.at[c])
 
+    small = [pltpu.make_async_copy(src, dst, small_sem.at[i]) for i, (src, dst) in enumerate(
+        ((w_key_in, w_key), (w_query_in, w_query), (gain_in, gain), (conv_in, conv)))]
+    for copy in small:
+        copy.start()
     for c in order:
         load(c).start()
 
@@ -43,6 +47,8 @@
     for j in range(1, n):
         greet(lax.rem(me + j, n))
 
+    for copy in small:
+        copy.wait()
     scale = gain[...].astype(F32).reshape(1, width)
     wcat[pl.ds(0, rank), :] = (w_key[...].astype(F32) * scale).astype(BF16)
     wcat[pl.ds(rank, rank), :] = (w_query[...].astype(F32) * scale).astype(BF16)
@@ -84,29 +90,33 @@
     kbuf[...] = summed.astype(BF16)
     keys_t = summed.T.astype(BF16)
 
-    for p in range(team):
-        own[p] = jnp.dot(keys_t, hbuf[:, p * part:(p + 1) * part], preferred_element_type=F32).astype(BF16)
-
-    def phase1(j):
+    def phase1(j, c):
         to = lax.rem(pos + j, team)
         return pltpu.make_async_remote_copy(
-            src_ref=own.at[to], dst_ref=got.at[pos], send_sem=send1.at[j - 1], recv_sem=recv1.at[j - 1],
+            src_ref=own.at[to * pieces + c], dst_ref=got.at[pos * pieces + c],
+            send_sem=send1.at[j - 1, c], recv_sem=recv1.at[j - 1, c],
             device_id={"seq": plane * team + to}, device_id_type=MESH)
 
-    def phase2(k):
+    def phase2(k, c):
         return pltpu.make_async_remote_copy(
-            src_ref=total, dst_ref=got2.at[k - 1], send_sem=send2.at[k - 1], recv_sem=recv2.at[k - 1],
+            src_ref=total.at[c], dst_ref=got2.at[k - 1, c],
+            send_sem=send2.at[k - 1, c], recv_sem=recv2.at[k - 1, c],
             device_id={"seq": lax.rem(plane + k, planes) * team + pos}, device_id_type=MESH)
 
-    def phase3(j):
+    def phase3(j, c):
         to = lax.rem(pos + j, team)
         return pltpu.make_async_remote_copy(
-            src_ref=pbuf.at[to], dst_ref=pref_out.at[pos], send_sem=send3.at[j - 1], recv_sem=recv3.at[j - 1],
+            src_ref=pbuf.at[to * pieces + c], dst_ref=pref_out.at[pos * pieces + c],
+            send_sem=send3.at[j - 1, c], recv_sem=recv3.at[j - 1, c],
             device_id={"seq": plane * team + to}, device_id_type=MESH)
 
-    for j in range(1, team):
-        phase1(j).start()
-    got[pos] = own[pos]
+    for c in range(pieces):
+        for p in range(team):
+            at = p * pieces + c
+            own[at] = jnp.dot(keys_t, hbuf[:, at * part:(at + 1) * part], preferred_element_type=F32).astype(BF16)
+        for j in range(1, team):
+            phase1(j, c).start()
+        got[pos * pieces + c] = own[pos * pieces + c]
 
     q = qbuf[...]
     q_out[...] = q
@@ -131,37 +141,41 @@
 
     local(0)
 
-    for j in range(1, team):
-        phase1(j).wait()
-    total[...] = sum(got[p].astype(F32) for p in range(team)).astype(BF16)
-    for k in range(1, planes):
-        @pl.when(plane + k < planes)
-        def _():
-            phase2(k).start()
+    for c in range(pieces):
+        for j in range(1, team):
+            phase1(j, c).wait()
+        total[c] = sum(got[p * pieces + c].astype(F32) for p in range(team)).astype(BF16)
+        for k in range(1, planes):
+            @pl.when(plane + k < planes)
+            def _():
+                phase2(k, c).start()
 
     local(1)
 
-    acc[...] = jnp.zeros_like(acc)
-    for k in range(1, planes):
-        @pl.when(plane >= k)
-        def _():
-            phase2(k).wait_recv()
-            acc[...] += got2[k - 1].astype(F32)
-
-    running = acc[...]
-    for p in range(team):
-        pbuf[p] = running.astype(BF16)
-        if p < team - 1:
-            running = running + got[p].astype(F32)
-    for j in range(1, team):
-        phase3(j).start()
-    pref_out[pos] = pbuf[pos]
-    for j in range(1, team):
-        phase3(j).wait()
-    for k in range(1, planes):
-        @pl.when(plane + k < planes)
-        def _():
-            phase2(k).wait_send()
+    for c in range(pieces):
+        acc[...] = jnp.zeros_like(acc)
+        for k in range(1, planes):
+            @pl.when(plane >= k)
+            def _():
+                phase2(k, c).wait_recv()
+                acc[...] += got2[k - 1, c].astype(F32)
+
+        running = acc[...]
+        for p in range(team):
+            pbuf[p * pieces + c] = running.astype(BF16)
+            if p < team - 1:
+                running = running + got[p * pieces + c].astype(F32)
+        for j in range(1, team):
+            phase3(j, c).start()
+        pref_out[pos * pieces + c] = pbuf[pos * pieces + c]
+
+    for c in range(pieces):
+        for j in range(1, team):
+            phase3(j, c).wait()
+        for k in range(1, planes):
+            @pl.when(plane + k < planes)
+            def _():
+                phase2(k, c).wait_send()
 
     @pl.when(me < n - 1)
     def _():
@@ -196,21 +210,26 @@
     taps, rank = conv_kernel.shape
     team = 4
     planes = n // team
-    part = width // team
+    pieces = 2
+    part = width // (team * pieces)
     chunks = 4
     vmem = pl.BlockSpec(memory_space=pltpu.VMEM)
     anyspace = pl.BlockSpec(memory_space=pltpu.HBM)
     dma = pltpu.SemaphoreType.DMA
     later = max(planes - 1, 1)
     local, q, pref = pl.pallas_call(
-        functools.partial(state_kernel, n, team),
+        functools.partial(state_kernel, n, team, pieces),
         out_shape=(jax.ShapeDtypeStruct((rows, width), F32),
                    jax.ShapeDtypeStruct((rows, rank), BF16),
-                   jax.ShapeDtypeStruct((team, rank, part), BF16)),
-        in_specs=[anyspace, vmem, vmem, vmem, vmem],
+                   jax.ShapeDtypeStruct((team * pieces, rank, part), BF16)),
+        in_specs=[anyspace] * 5,
         out_specs=(vmem, vmem, vmem),
         scratch_shapes=[
             pltpu.VMEM((rows, width), BF16),
+            pltpu.VMEM((width,), BF16),
+            pltpu.VMEM((rank, width), BF16),
+            pltpu.VMEM((rank, width), BF16),
+            pltpu.VMEM((taps, rank), F32),
             pltpu.VMEM((2 * rank, width), BF16),
             pltpu.VMEM((rows + 8, rank), F32),
             pltpu.VMEM((8, 128), F32),
@@ -218,20 +237,21 @@
             pltpu.VMEM((rows, rank), BF16),
             pltpu.VMEM((rows, rank), BF16),
             pltpu.VMEM((rows, rows), BF16),
-            pltpu.VMEM((team, rank, part), BF16),
-            pltpu.VMEM((team, rank, part), BF16),
-            pltpu.VMEM((rank, part), BF16),
-            pltpu.VMEM((later, rank, part), BF16),
+            pltpu.VMEM((team * pieces, rank, part), BF16),
+            pltpu.VMEM((team * pieces, rank, part), BF16),
+            pltpu.VMEM((pieces, rank, part), BF16),
+            pltpu.VMEM((later, pieces, rank, part), BF16),
             pltpu.VMEM((rank, part), F32),
-            pltpu.VMEM((team, rank, part), BF16),
-            dma((chunks,)), dma((2,)),
-            dma((team - 1,)), dma((team - 1,)),
-            dma((later,)), dma((later,)),
-            dma((team - 1,)), dma((team - 1,)),
+            pltpu.VMEM((team * pieces, rank, part), BF16),
+            dma((4,)), dma((chunks,)), dma((2,)),
+            dma((team - 1, pieces)), dma((team - 1, pieces)),
+            dma((later, pieces)), dma((later, pieces)),
+            dma((team - 1, pieces)), dma((team - 1, pieces)),
         ],
         compiler_params=pltpu.CompilerParams(
             collective_id=0, has_side_effects=True, vmem_limit_bytes=32 * 1024 * 1024),
-    )(hidden, norm_gain, w_key.T, w_query.T, conv_kernel)
+    )(*(pltpu.with_memory_space_constraint(x, pltpu.HBM) for x in (
+        hidden, norm_gain, w_key.T, w_query.T, conv_kernel)))
 
     return pl.pallas_call(
         finish_kernel,

time: 32.5 us -> 24.2 us (0.74)
  local copies, waits for them, and re-layouts: 5.47 us -> 0.01 us
  Pallas kernels: 26.8 us -> 24 us
    unnamed x12 -> x2, local copies, waits for them, and re-layouts: 5.47 us -> 0.01 us
    pallas_call x1, Pallas kernels: 23.4 us -> 20.8 us  [shards(): pl.pallas_call(functools.partial(state_kernel, n, team, pieces), out_shap...]
where the time goes in v2:
time: 24.2 us; the launch traced here: 24.1 us
  Pallas kernels  24 us (99%)
    pallas_call x1, Pallas kernels, shards(): pl.pallas_call(functools.partial(state_kernel, n, team, pieces), out_shap...  20.8 us
    pallas_call x1, Pallas kernels, shards(): pl.pallas_call(finish_kernel, out_shape=jax.ShapeDtypeStruct((rows, width...  3.21 us

profile of v2, /device:TPU:25, one launch (start us, length us, event | category | flops | bytes accessed | tf_op | source)
XLA Modules:
  0.0 24.1 jit_solution(9507432077002930028)
XLA Ops:
  0.0 0.0 copy-start
  0.0 20.8 %shard_map.64 = (f32[512,4096]{1,0:T(8,128)S(1)}, bf16[512,32]{1,0:T(8,128)(2,1)S(1)}, bf16[8,32,512]{2,1,0:T(8,128)(2,1)S(1)}) custom-call(bf16[512,4096]{1,0:T(8,128)(2,1)} %hidden.1, bf16[4096]{0:T(1024)(128)(2,1)} %gain_in.1, bf16[32,4096]{1,0:T(8,128)(2,1)} %bitcast.2, bf16[32,4096]{1,0:T(8,128)(2,1)} %bitcast.3, f32[4,32]{1,0:T(4,128)} %conv_in.1), custom_call_target="tpu_custom_call" | custom-call | tf_op jit(solution)/shard_map/pallas_call | solution.py:220
  20.8 0.0 copy-done
  20.8 3.2 %shard_map.65 = bf16[512,4096]{1,0:T(8,128)(2,1)} custom-call(f32[512,4096]{1,0:T(8,128)S(1)} %get-tuple-element.8.local, bf16[512,32]{1,0:T(8,128)(2,1)S(1)} %get-tuple-element.9.q, bf16[8,32,512]{2,1,0:T(8,128)(2,1)S(1)} %get-tuple-element.10.pref, bf16[4096]{0:T(1024)(128)(2,1)S(1)} %copy-done), custom_call_target="tpu_custom_call" | custom-call | tf_op jit(solution)/shard_map/pallas_call | solution.py:256
Async XLA Ops:
  0.0 20.8 %copy-start = (bf16[4096]{0:T(1024)(128)(2,1)S(1)}, bf16[4096]{0:T(1024)(128)(2,1)}, u32[]{:S(2)}) copy-start(bf16[4096]{0:T(1024)(128)(2,1)} %gain.1) | copy-start | bytes 24580

commit v3 on v2

--- a/solution.py
+++ b/solution.py
@@ -13,8 +13,8 @@
 BF16 = jnp.bfloat16
 
 
-def state_kernel(n, team, pieces, hidden, gain_in, w_key_in, w_query_in, conv_in, local_out, q_out, pref_out,
-                 hbuf, gain, w_key, w_query, conv, wcat, rk, tail, halo, kbuf, qbuf, sbuf, own, got, total, got2, acc, pbuf,
+def state_kernel(n, team, pieces, hidden, gain_in, w_key_in, w_query_in, conv_in, mixed, inv_out,
+                 pref, squares, hbuf, gain, w_key, w_query, conv, wcat, rk, tail, halo, kbuf, qbuf, sbuf, own, got, total, got2, acc, pbuf,
                  small_sem, load_sem, halo_sem, send1, recv1, send2, recv2, send3, recv3):
     rows, width = hbuf.shape
     rank = w_key.shape[0]
@@ -26,6 +26,14 @@
     me = lax.axis_index("seq")
     pos = lax.rem(me, team)
     plane = me // team
+    rounds = (planes - 1).bit_length()
+
+    def takes(r):
+        return lax.rem(plane // 2 ** r, 2) == 1
+
+    def gives(r, k):
+        return (lax.rem(plane, 2 ** (r + 1)) == 2 ** r - 1) & (plane + k < planes)
+
     order = [chunks - 1] + list(range(chunks - 1))
 
     def load(c):
@@ -44,8 +52,17 @@
     def greet(other):
         pl.semaphore_signal(barrier, inc=1, device_id={"seq": other}, device_id_type=MESH)
 
-    for j in range(1, n):
-        greet(lax.rem(me + j, n))
+    for j in range(1, team):
+        greet(plane * team + lax.rem(pos + j, team))
+
+    @pl.when((pos == 0) & (me > 0))
+    def _():
+        greet(me - 1)
+
+    for r in range(rounds):
+        @pl.when(takes(r))
+        def _():
+            greet((plane // 2 ** r * 2 ** r - 1) * team + pos)
 
     for copy in small:
         copy.wait()
@@ -69,7 +86,11 @@
         if c == chunks - 1:
             tail[:, :rank] = keys[step - 8:, :]
             tail[:, rank:] = jnp.zeros((8, tail.shape[1] - rank), F32)
-            pl.semaphore_wait(barrier, n - 1)
+            peers = team - 1 + ((pos == team - 1) & (me < n - 1)).astype(jnp.int32)
+            for r in range(rounds):
+                for k in range(1, 2 ** r + 1):
+                    peers = peers + gives(r, k).astype(jnp.int32)
+            pl.semaphore_wait(barrier, peers)
 
             @pl.when(me < n - 1)
             def _():
@@ -97,16 +118,23 @@
             send_sem=send1.at[j - 1, c], recv_sem=recv1.at[j - 1, c],
             device_id={"seq": plane * team + to}, device_id_type=MESH)
 
-    def phase2(k, c):
+    def phase2(r, k, c):
+        slot = 2 ** r - 2 + k
         return pltpu.make_async_remote_copy(
-            src_ref=total.at[c], dst_ref=got2.at[k - 1, c],
-            send_sem=send2.at[k - 1, c], recv_sem=recv2.at[k - 1, c],
+            src_ref=total.at[r, c], dst_ref=got2.at[r, c],
+            send_sem=send2.at[slot, c], recv_sem=recv2.at[r, c],
             device_id={"seq": lax.rem(plane + k, planes) * team + pos}, device_id_type=MESH)
+
+    def pass_on(r, c):
+        for k in range(1, 2 ** r + 1):
+            @pl.when(gives(r, k))
+            def _():
+                phase2(r, k, c).start()
 
     def phase3(j, c):
         to = lax.rem(pos + j, team)
         return pltpu.make_async_remote_copy(
-            src_ref=pbuf.at[to * pieces + c], dst_ref=pref_out.at[pos * pieces + c],
+            src_ref=pbuf.at[to * pieces + c], dst_ref=pref.at[pos * pieces + c],
             send_sem=send3.at[j - 1, c], recv_sem=recv3.at[j - 1, c],
             device_id={"seq": plane * team + to}, device_id_type=MESH)
 
@@ -119,7 +147,6 @@
         got[pos * pieces + c] = own[pos * pieces + c]
 
     q = qbuf[...]
-    q_out[...] = q
     scores = lax.dot_general(q, kbuf[...], (((1,), (1,)), ((), ())), preferred_element_type=F32)
     at_row = lax.broadcasted_iota(jnp.int32, scores.shape, 0)
     at_col = lax.broadcasted_iota(jnp.int32, scores.shape, 1)
@@ -129,76 +156,96 @@
     half = rows // halves
     tile = 512
 
-    def local(b):
+    def local(b, first, last):
         depth = (b + 1) * half
 
-        @pl.loop(0, width // tile)
+        @pl.loop(first, last)
         def _(t):
             cols = pl.ds(pl.multiple_of(t * tile, tile), tile)
-            local_out[pl.ds(b * half, half), cols] = jnp.dot(
+            mixed[pl.ds(b * half, half), cols] = jnp.dot(
                 sbuf[pl.ds(b * half, half), pl.ds(0, depth)], hbuf[pl.ds(0, depth), cols],
                 preferred_element_type=F32)
 
-    local(0)
-
+    tiles = width // tile
+    local(0, 0, tiles)
     for c in range(pieces):
         for j in range(1, team):
             phase1(j, c).wait()
-        total[c] = sum(got[p * pieces + c].astype(F32) for p in range(team)).astype(BF16)
-        for k in range(1, planes):
-            @pl.when(plane + k < planes)
-            def _():
-                phase2(k, c).start()
-
-    local(1)
-
-    for c in range(pieces):
-        acc[...] = jnp.zeros_like(acc)
-        for k in range(1, planes):
-            @pl.when(plane >= k)
-            def _():
-                phase2(k, c).wait_recv()
-                acc[...] += got2[k - 1, c].astype(F32)
-
-        running = acc[...]
+        total[0, c] = sum(got[p * pieces + c].astype(F32) for p in range(team)).astype(BF16)
+        pass_on(0, c)
+        acc[c] = jnp.zeros(acc.shape[1:], F32)
+
+    local(1, 0, tiles // 2)
+
+    def send_back(c):
+        running = acc[c]
         for p in range(team):
             pbuf[p * pieces + c] = running.astype(BF16)
             if p < team - 1:
                 running = running + got[p * pieces + c].astype(F32)
         for j in range(1, team):
             phase3(j, c).start()
-        pref_out[pos * pieces + c] = pbuf[pos * pieces + c]
-
+        pref[pos * pieces + c] = pbuf[pos * pieces + c]
+
+    for r in range(rounds):
+        for c in range(pieces):
+            @pl.when(takes(r))
+            def _():
+                phase2(r, 1, c).wait_recv()
+                acc[c] += got2[r, c].astype(F32)
+
+            if r + 1 < rounds:
+                total[r + 1, c] = (acc[c] + total[0, c].astype(F32)).astype(BF16)
+                pass_on(r + 1, c)
+            else:
+                send_back(c)
+        if r == 0 and rounds > 1:
+            local(1, tiles // 2, tiles)
+    if rounds == 0:
+        for c in range(pieces):
+            send_back(c)
+    if rounds < 2:
+        local(1, tiles // 2, tiles)
+
+    squares[...] = jnp.zeros_like(squares)
+    band = 128
     for c in range(pieces):
         for j in range(1, team):
             phase3(j, c).wait()
-        for k in range(1, planes):
-            @pl.when(plane + k < planes)
-            def _():
-                phase2(k, c).wait_send()
+
+        @pl.loop(0, rows // band)
+        def _(t):
+            span = pl.ds(pl.multiple_of(t * band, band), band)
+            for p in range(team):
+                at = p * pieces + c
+                cols = pl.ds(at * part, part)
+                m = mixed[span, cols] + jnp.dot(qbuf[span, :], pref[at], preferred_element_type=F32)
+                mixed[span, cols] = m
+                m = m * m
+                squares[span, :] += sum(m[:, i:i + 128] for i in range(0, part, 128))
+
+    inv_out[...] = lax.rsqrt(jnp.sum(squares[...], axis=1, keepdims=True) * (1.0 / width) + epsilon)
+    for c in range(pieces):
+        for r in range(rounds):
+            for k in range(1, 2 ** r + 1):
+                @pl.when(gives(r, k))
+                def _():
+                    phase2(r, k, c).wait_send()
 
     @pl.when(me < n - 1)
     def _():
         halo_copy.wait_send()
 
 
-def finish_kernel(local, q, pref, gain, out, mixed, done, sem):
-    team, _, part = pref.shape
-    width = team * part
+def finish_kernel(mixed, inv, gain, out, done, sem):
+    rows, width = mixed.shape
     blocks = sem.shape[0]
-    block = local.shape[0] // blocks
+    block = rows // blocks
     scale = gain[...].astype(F32).reshape(1, width)
     copies = []
     for b in range(blocks):
         span = pl.ds(b * block, block)
-        squares = jnp.zeros((block, 1), F32)
-        for p in range(team):
-            cols = pl.ds(p * part, part)
-            m = local[span, cols] + jnp.dot(q[span, :], pref[p], preferred_element_type=F32)
-            mixed[:, cols] = m
-            squares = squares + jnp.sum(m * m, axis=1, keepdims=True)
-        inv = lax.rsqrt(squares * (1.0 / width) + epsilon)
-        done[span, :] = (mixed[...] * inv * scale).astype(BF16)
+        done[span, :] = (mixed[span, :] * inv[span, :] * scale).astype(BF16)
         copies.append(pltpu.make_async_copy(done.at[span], out.at[span], sem.at[b]))
         copies[-1].start()
     for copy in copies:
@@ -212,19 +259,21 @@
     planes = n // team
     pieces = 2
     part = width // (team * pieces)
-    chunks = 4
+    chunks = 2
     vmem = pl.BlockSpec(memory_space=pltpu.VMEM)
     anyspace = pl.BlockSpec(memory_space=pltpu.HBM)
     dma = pltpu.SemaphoreType.DMA
-    later = max(planes - 1, 1)
-    local, q, pref = pl.pallas_call(
+    rounds = max((planes - 1).bit_length(), 1)
+    slots = max(2 ** rounds - 1, 1)
+    mixed, inv = pl.pallas_call(
         functools.partial(state_kernel, n, team, pieces),
         out_shape=(jax.ShapeDtypeStruct((rows, width), F32),
-                   jax.ShapeDtypeStruct((rows, rank), BF16),
-                   jax.ShapeDtypeStruct((team * pieces, rank, part), BF16)),
+                   jax.ShapeDtypeStruct((rows, 1), F32)),
         in_specs=[anyspace] * 5,
-        out_specs=(vmem, vmem, vmem),
+        out_specs=(vmem, vmem),
         scratch_shapes=[
+            pltpu.VMEM((team * pieces, rank, part), BF16),
+            pltpu.VMEM((rows, 128), F32),
             pltpu.VMEM((rows, width), BF16),
             pltpu.VMEM((width,), BF16),
             pltpu.VMEM((rank, width), BF16),
@@ -239,13 +288,13 @@
             pltpu.VMEM((rows, rows), BF16),
             pltpu.VMEM((team * pieces, rank, part), BF16),
             pltpu.VMEM((team * pieces, rank, part), BF16),
-            pltpu.VMEM((pieces, rank, part), BF16),
-            pltpu.VMEM((later, pieces, rank, part), BF16),
-            pltpu.VMEM((rank, part), F32),
+            pltpu.VMEM((rounds, pieces, rank, part), BF16),
+            pltpu.VMEM((rounds, pieces, rank, part), BF16),
+            pltpu.VMEM((pieces, rank, part), F32),
             pltpu.VMEM((team * pieces, rank, part), BF16),
             dma((4,)), dma((chunks,)), dma((2,)),
             dma((team - 1, pieces)), dma((team - 1, pieces)),
-            dma((later, pieces)), dma((later, pieces)),
+            dma((slots, pieces)), dma((rounds, pieces)),
             dma((team - 1, pieces)), dma((team - 1, pieces)),
         ],
         compiler_params=pltpu.CompilerParams(
@@ -256,11 +305,11 @@
     return pl.pallas_call(
         finish_kernel,
         out_shape=jax.ShapeDtypeStruct((rows, width), BF16),
-        in_specs=[vmem, vmem, vmem, vmem],
+        in_specs=[vmem, vmem, vmem],
         out_specs=anyspace,
-        scratch_shapes=[pltpu.VMEM((rows // 8, width), F32), pltpu.VMEM((rows, width), BF16), dma((8,))],
+        scratch_shapes=[pltpu.VMEM((rows, width), BF16), dma((8,))],
         compiler_params=pltpu.CompilerParams(vmem_limit_bytes=32 * 1024 * 1024),
-    )(local, q, pref, out_gain)
+    )(mixed, inv, out_gain)
 
 
 def solution(mesh):

time: 24.2 us -> 22.6 us (0.934)
  Pallas kernels: 24 us -> 22.4 us
    pallas_call x1, Pallas kernels: 3.21 us -> 2.23 us  [shards(): pl.pallas_call(finish_kernel, out_shape=jax.ShapeDtypeStruct((rows, width...]
    pallas_call x1, Pallas kernels: 20.8 us -> 20.2 us  [shards(): pl.pallas_call(functools.partial(state_kernel, n, team, pieces), out_shap...]
where the time goes in v3:
time: 22.6 us; the launch traced here: 22.4 us
  Pallas kernels  22.4 us (99%)
    pallas_call x1, Pallas kernels, shards(): pl.pallas_call(functools.partial(state_kernel, n, team, pieces), out_shap...  20.2 us
    pallas_call x1, Pallas kernels, shards(): pl.pallas_call(finish_kernel, out_shape=jax.ShapeDtypeStruct((rows, width...  2.23 us

profile of v3, /device:TPU:25, one launch (start us, length us, event | category | flops | bytes accessed | tf_op | source)
XLA Modules:
  0.0 22.4 jit_solution(8508117492162681426)
XLA Ops:
  0.0 0.0 copy-start
  0.0 20.2 %shard_map.64 = (f32[512,4096]{1,0:T(8,128)S(1)}, f32[512,1]{1,0:T(8,128)S(1)}) custom-call(bf16[512,4096]{1,0:T(8,128)(2,1)} %hidden.1, bf16[4096]{0:T(1024)(128)(2,1)} %gain_in.1, bf16[32,4096]{1,0:T(8,128)(2,1)} %bitcast.2, bf16[32,4096]{1,0:T(8,128)(2,1)} %bitcast.3, f32[4,32]{1,0:T(4,128)} %conv_in.1), custom_call_target="tpu_custom_call" | custom-call | tf_op jit(solution)/shard_map/pallas_call | solution.py:268
  20.2 0.0 copy-done
  20.2 2.2 %shard_map.65 = bf16[512,4096]{1,0:T(8,128)(2,1)} custom-call(f32[512,4096]{1,0:T(8,128)S(1)} %get-tuple-element.7.mixed, f32[512,1]{1,0:T(8,128)S(1)} %get-tuple-element.8.inv, bf16[4096]{0:T(1024)(128)(2,1)S(1)} %copy-done), custom_call_target="tpu_custom_call" | custom-call | tf_op jit(solution)/shard_map/pallas_call | solution.py:305
Async XLA Ops:
  0.0 20.2 %copy-start = (bf16[4096]{0:T(1024)(128)(2,1)S(1)}, bf16[4096]{0:T(1024)(128)(2,1)}, u32[]{:S(2)}) copy-start(bf16[4096]{0:T(1024)(128)(2,1)} %gain.1) | copy-start | bytes 24580

commit v4 on v3

--- a/solution.py
+++ b/solution.py
@@ -208,7 +208,7 @@
         local(1, tiles // 2, tiles)
 
     squares[...] = jnp.zeros_like(squares)
-    band = 128
+    band = 256
     for c in range(pieces):
         for j in range(1, team):
             phase3(j, c).wait()

time: 22.6 us -> 22.1 us (0.978)
  Pallas kernels: 22.4 us -> 21.9 us
    pallas_call x1, Pallas kernels: 20.2 us -> 19.7 us  [shards(): pl.pallas_call(functools.partial(state_kernel, n, team, pieces), out_shap...]
where the time goes in v4:
time: 22.1 us; the launch traced here: 21.9 us
  Pallas kernels  21.9 us (99%)
    pallas_call x1, Pallas kernels, shards(): pl.pallas_call(functools.partial(state_kernel, n, team, pieces), out_shap...  19.7 us
    pallas_call x1, Pallas kernels, shards(): pl.pallas_call(finish_kernel, out_shape=jax.ShapeDtypeStruct((rows, width...  2.23 us

profile of v4, /device:TPU:25, one launch (start us, length us, event | category | flops | bytes accessed | tf_op | source)
XLA Modules:
  0.0 21.9 jit_solution(6328475717279226921)
XLA Ops:
  0.0 0.0 copy-start
  0.0 19.7 %shard_map.64 = (f32[512,4096]{1,0:T(8,128)S(1)}, f32[512,1]{1,0:T(8,128)S(1)}) custom-call(bf16[512,4096]{1,0:T(8,128)(2,1)} %hidden.1, bf16[4096]{0:T(1024)(128)(2,1)} %gain_in.1, bf16[32,4096]{1,0:T(8,128)(2,1)} %bitcast.2, bf16[32,4096]{1,0:T(8,128)(2,1)} %bitcast.3, f32[4,32]{1,0:T(4,128)} %conv_in.1), custom_call_target="tpu_custom_call" | custom-call | tf_op jit(solution)/shard_map/pallas_call | solution.py:268
  19.7 0.0 copy-done
  19.7 2.2 %shard_map.65 = bf16[512,4096]{1,0:T(8,128)(2,1)} custom-call(f32[512,4096]{1,0:T(8,128)S(1)} %get-tuple-element.7.mixed, f32[512,1]{1,0:T(8,128)S(1)} %get-tuple-element.8.inv, bf16[4096]{0:T(1024)(128)(2,1)S(1)} %copy-done), custom_call_target="tpu_custom_call" | custom-call | tf_op jit(solution)/shard_map/pallas_call | solution.py:305
Async XLA Ops:
  0.0 19.7 %copy-start = (bf16[4096]{0:T(1024)(128)(2,1)S(1)}, bf16[4096]{0:T(1024)(128)(2,1)}, u32[]{:S(2)}) copy-start(bf16[4096]{0:T(1024)(128)(2,1)} %gain.1) | copy-start | bytes 24580
